TPU v7x, 32 devices: a whole 2x2x4 slice. The times are simulated.
32 devices in a mesh: dp: 8 (over z, y), tensor: 4 (over x, core).
Axes of the slice: x: 2, y: 2, z: 4, core: 2. Of those that a mesh axis runs over, the one named last changes fastest.
Arguments:
- tokens: bfloat16 [16384, 1536], P(('dp', 'tensor')), may hold values from -6 to 6
- segments: int32 [16384], P('dp'), may hold values from 0 to 3, as said below
- positions: int32 [16384], P('dp'), may hold values from 0 to 2044, as said below
- norm_attn: float32 [1536], replicated, may hold values from 0.1 to 1.9
- w_query: bfloat16 [1536, 1536], P(None, 'tensor'), may hold values from -0.15625 to 0.15625
- key_weight: bfloat16 [1536, 768], P(None, 'tensor'), may hold values from -0.15625 to 0.15625
- value_weight: bfloat16 [1536, 768], P(None, 'tensor'), may hold values from -0.15625 to 0.15625
- w_out: bfloat16 [1536, 1536], P('tensor'), may hold values from -1.5 to 1.5
- norm_mlp: float32 [1536], replicated, may hold values from 0.1 to 1.9
- w_gate: bfloat16 [1536, 4096], P(None, 'tensor'), may hold values from -0.15625 to 0.15625
- w_up: bfloat16 [1536, 4096], P(None, 'tensor'), may hold values from -0.15625 to 0.15625
- w_down: bfloat16 [4096, 1536], P('tensor'), may hold values from -0.09375 to 0.09375
- cotangent: bfloat16 [16384, 1536], P(('dp', 'tensor')), may hold values from -6 to 6
Outputs:
- output: bfloat16 [16384, 1536], P(('dp', 'tensor'))
- grad_tokens: float32 [16384, 1536], P(('dp', 'tensor'))
- grad_norm_attn: float32 [1536], replicated
- grad_w_query: float32 [1536, 1536], P(None, 'tensor')
- grad_w_key: float32 [1536, 768], P(None, 'tensor')
- grad_w_value: float32 [1536, 768], P(None, 'tensor')
- grad_w_out: float32 [1536, 1536], P('tensor')
- grad_norm_mlp: float32 [1536], replicated
- grad_w_gate: float32 [1536, 4096], P(None, 'tensor')
- grad_w_up: float32 [1536, 4096], P(None, 'tensor')
- grad_w_down: float32 [4096, 1536], P('tensor')
Inputs may be any that keep to these rules, and one draw needn't show every extreme that they name: `segments`: within each sequence of 2048 tokens the document numbers never fall, start at 0 and end at 3, each document one token or more. `positions`: each token's position within its document, 0 at the document's first token; the first sequence holds a document of 2045 tokens.
All inputs are finite; a program needn't handle non-finite values.
Results may differ from a plain program's by a relative error of at most 0.018.
Values may be sent and summed in bfloat16 or wider, within the bound.
A program may use at most 256 MiB of HBM per device.

v0:
```python
import math
import jax
import jax.numpy as jnp
from jax import lax
from jax.sharding import PartitionSpec as P

HEAD_SIZE = 96
epsilon = 1e-05
rope_base = 100000.0
masked_value = -1e30


def angle_tables(positions, width):
    middle = width // 2
    freq_steps = jnp.arange(middle, dtype=jnp.float32)
    inverse = jnp.exp(freq_steps * (-2.0 * math.log(rope_base) / width))
    angles = positions.astype(jnp.float32)[:, None] * inverse[None, :]
    return (jnp.cos(angles)[:, None, :], jnp.sin(angles)[:, None, :])


def apply_rotary(values, cosine_lookup, sine_lookup):
    middle = values.shape[-1] // 2
    front, second = (values[..., :middle], values[..., middle:])
    return jnp.concatenate(
        [
            front * cosine_lookup - second * sine_lookup,
            second * cosine_lookup + front * sine_lookup,
        ],
        axis=-1,
    )


def rotate_back(grads_in, cosine_lookup, sine_lookup):
    middle = grads_in.shape[-1] // 2
    front, second = (grads_in[..., :middle], grads_in[..., middle:])
    return jnp.concatenate(
        [
            front * cosine_lookup + second * sine_lookup,
            second * cosine_lookup - front * sine_lookup,
        ],
        axis=-1,
    )


def rms_inverse(values):
    return lax.rsqrt(jnp.mean(values * values, axis=-1, keepdims=True) + epsilon)


def norm_back(grad_normed, gain, unit_rows, inverse):
    scaled = grad_normed * gain
    return inverse * (scaled - unit_rows * jnp.mean(scaled * unit_rows, axis=-1, keepdims=True))


def contract_rows(left, right):
    return lax.dot_general(
        left, right, (((0,), (0,)), ((), ())), preferred_element_type=jnp.float32
    )


def contract_cols(left, right):
    return lax.dot_general(
        left, right, (((1,), (1,)), ((), ())), preferred_element_type=jnp.float32
    )


def block_scores(query_block, heads_of_key, allowed, score_scale):
    scores = (
        jnp.einsum("qgrd,kgd->grqk", query_block, heads_of_key, preferred_element_type=jnp.float32)
        * score_scale
    )
    return jnp.where(allowed[None, None], scores, masked_value)


def body(
    tokens,
    segments,
    positions,
    norm_attn,
    w_query,
    key_weight,
    value_weight,
    w_out,
    norm_mlp,
    w_gate,
    w_up,
    w_down,
    cotangent,
):
    sequence_length = segments.shape[0]
    q_heads = w_query.shape[1] // HEAD_SIZE
    kv_heads = key_weight.shape[1] // HEAD_SIZE
    head_repetitions = q_heads // kv_heads
    score_scale = 1.0 / math.sqrt(HEAD_SIZE)
    rows_per_block = min(512, sequence_length)
    block_total = sequence_length // rows_per_block
    cosine_lookup, sine_lookup = angle_tables(positions, HEAD_SIZE)
    indices = jnp.arange(sequence_length, dtype=jnp.int32)
    seg_blocks = segments.reshape(block_total, rows_per_block)
    index_blocks = indices.reshape(block_total, rows_per_block)
    inputs = tokens.astype(jnp.float32)
    inverse_one = rms_inverse(inputs)
    unit_one = inputs * inverse_one
    first_normalized = (unit_one * norm_attn).astype(jnp.bfloat16)
    attn_in = lax.all_gather(first_normalized, "tensor", axis=0, tiled=True)
    query_proj = jnp.dot(attn_in, w_query, preferred_element_type=jnp.float32).reshape(
        sequence_length, q_heads, HEAD_SIZE
    )
    key_proj = jnp.dot(attn_in, key_weight, preferred_element_type=jnp.float32).reshape(
        sequence_length, kv_heads, HEAD_SIZE
    )
    query_rows = apply_rotary(query_proj, cosine_lookup, sine_lookup).astype(jnp.bfloat16)
    heads_of_key = apply_rotary(key_proj, cosine_lookup, sine_lookup).astype(jnp.bfloat16)
    heads_of_value = (
        jnp.dot(attn_in, value_weight, preferred_element_type=jnp.float32)
        .astype(jnp.bfloat16)
        .reshape(sequence_length, kv_heads, HEAD_SIZE)
    )
    blocks_of_query = query_rows.reshape(
        block_total, rows_per_block, kv_heads, head_repetitions, HEAD_SIZE
    )

    def attend(member):
        query_block, rows_seg, rows_idx = member
        allowed = (rows_seg[:, None] == segments[None, :]) & (indices[None, :] <= rows_idx[:, None])
        scores = block_scores(query_block, heads_of_key, allowed, score_scale)
        row_peak = jnp.max(scores, axis=-1, keepdims=True)
        weights = jnp.exp(scores - row_peak)
        totals = jnp.sum(weights, axis=-1, keepdims=True)
        weights_low = (weights / totals).astype(jnp.bfloat16)
        mixed_heads = jnp.einsum(
            "grqk,kgd->qgrd", weights_low, heads_of_value, preferred_element_type=jnp.float32
        )
        return (mixed_heads.astype(jnp.bfloat16), row_peak[..., 0] + jnp.log(totals[..., 0]))

    attended, log_totals = lax.map(attend, (blocks_of_query, seg_blocks, index_blocks))
    attended = attended.reshape(sequence_length, q_heads * HEAD_SIZE)
    row_slice = attended
    attn_out = lax.psum_scatter(
        jnp.dot(row_slice, w_out, preferred_element_type=jnp.float32),
        "tensor",
        scatter_dimension=0,
        tiled=True,
    )
    hidden_one = inputs + attn_out
    inverse_two = rms_inverse(hidden_one)
    unit_two = hidden_one * inverse_two
    normed_two = (unit_two * norm_mlp).astype(jnp.bfloat16)
    mlp_in = lax.all_gather(normed_two, "tensor", axis=0, tiled=True)
    gate_proj = jnp.dot(mlp_in, w_gate, preferred_element_type=jnp.float32)
    up_proj = jnp.dot(mlp_in, w_up, preferred_element_type=jnp.float32)
    sigmoid_gate = jax.nn.sigmoid(gate_proj)
    activated = gate_proj * sigmoid_gate
    hidden = (activated * up_proj).astype(jnp.bfloat16)
    row_slice = hidden
    mlp_out = lax.psum_scatter(
        jnp.dot(row_slice, w_down, preferred_element_type=jnp.float32).astype(jnp.bfloat16),
        "tensor",
        scatter_dimension=0,
        tiled=True,
    ).astype(jnp.float32)
    output = (hidden_one + mlp_out).astype(jnp.bfloat16)
    grad_out = lax.all_gather(cotangent, "tensor", axis=0, tiled=True)
    grad_w_down = contract_rows(hidden, grad_out)
    grad_hidden = contract_cols(grad_out, w_down)
    grad_gate = (
        grad_hidden * up_proj * sigmoid_gate * (1.0 + gate_proj * (1.0 - sigmoid_gate))
    ).astype(jnp.bfloat16)
    grad_upper = (grad_hidden * activated).astype(jnp.bfloat16)
    grad_w_gate = contract_rows(mlp_in, grad_gate)
    grad_w_up = contract_rows(mlp_in, grad_upper)
    grad_normed_two = lax.psum_scatter(
        contract_cols(grad_gate, w_gate) + contract_cols(grad_upper, w_up),
        "tensor",
        scatter_dimension=0,
        tiled=True,
    )
    grad_norm_mlp = jnp.sum(grad_normed_two * unit_two, axis=0)
    grad_hidden_one = cotangent.astype(jnp.float32) + norm_back(
        grad_normed_two, norm_mlp, unit_two, inverse_two
    )
    grad_attn_rows = lax.all_gather(
        grad_hidden_one.astype(jnp.bfloat16), "tensor", axis=0, tiled=True
    )
    grad_w_out = contract_rows(attended, grad_attn_rows)
    grad_attended = contract_cols(grad_attn_rows, w_out).astype(jnp.bfloat16)
    grad_blocks = grad_attended.reshape(
        block_total, rows_per_block, kv_heads, head_repetitions, HEAD_SIZE
    )

    def attend_back(running, member):
        query_block, grad_block, rows_seg, rows_idx, log_block = member
        allowed = (rows_seg[:, None] == segments[None, :]) & (indices[None, :] <= rows_idx[:, None])
        scores = block_scores(query_block, heads_of_key, allowed, score_scale)
        weights = jnp.exp(scores - log_block[..., None])
        grad_weights = jnp.einsum(
            "qgrd,kgd->grqk", grad_block, heads_of_value, preferred_element_type=jnp.float32
        )
        inner_sum = jnp.sum(weights * grad_weights, axis=-1, keepdims=True)
        grad_scores = (weights * (grad_weights - inner_sum)).astype(jnp.bfloat16)
        grad_query = (
            jnp.einsum(
                "grqk,kgd->qgrd", grad_scores, heads_of_key, preferred_element_type=jnp.float32
            )
            * score_scale
        )
        grad_keys = (
            running[0]
            + jnp.einsum(
                "grqk,qgrd->kgd", grad_scores, query_block, preferred_element_type=jnp.float32
            )
            * score_scale
        )
        grad_values = running[1] + jnp.einsum(
            "grqk,qgrd->kgd",
            weights.astype(jnp.bfloat16),
            grad_block,
            preferred_element_type=jnp.float32,
        )
        return ((grad_keys, grad_values), grad_query)

    zero_state = jnp.zeros((sequence_length, kv_heads, HEAD_SIZE), jnp.float32)
    (grad_keys, grad_values), grad_queries = lax.scan(
        attend_back,
        (zero_state, zero_state),
        (blocks_of_query, grad_blocks, seg_blocks, index_blocks, log_totals),
    )
    grad_queries = grad_queries.reshape(sequence_length, q_heads, HEAD_SIZE)
    grad_q_proj = (
        rotate_back(grad_queries, cosine_lookup, sine_lookup)
        .reshape(sequence_length, q_heads * HEAD_SIZE)
        .astype(jnp.bfloat16)
    )
    grad_k_proj = (
        rotate_back(grad_keys, cosine_lookup, sine_lookup)
        .reshape(sequence_length, kv_heads * HEAD_SIZE)
        .astype(jnp.bfloat16)
    )
    grad_v_proj = grad_values.reshape(sequence_length, kv_heads * HEAD_SIZE).astype(jnp.bfloat16)
    grad_w_query = contract_rows(attn_in, grad_q_proj)
    grad_w_key = contract_rows(attn_in, grad_k_proj)
    grad_w_value = contract_rows(attn_in, grad_v_proj)
    grad_normed_one = lax.psum_scatter(
        (
            contract_cols(grad_q_proj, w_query)
            + contract_cols(grad_k_proj, key_weight)
            + contract_cols(grad_v_proj, value_weight)
        ).astype(jnp.bfloat16),
        "tensor",
        scatter_dimension=0,
        tiled=True,
    ).astype(jnp.float32)
    grad_norm_attn = jnp.sum(grad_normed_one * unit_one, axis=0)
    grad_tokens = grad_hidden_one + norm_back(grad_normed_one, norm_attn, unit_one, inverse_one)
    grad_norm_attn, grad_norm_mlp = lax.psum((grad_norm_attn, grad_norm_mlp), ("dp", "tensor"))
    grad_w_query, grad_w_key, grad_w_value, grad_w_out, grad_w_gate, grad_w_up, grad_w_down = (
        lax.psum(grad_w_query.astype(jnp.bfloat16), "dp").astype(jnp.float32),
        lax.psum(grad_w_key.astype(jnp.bfloat16), "dp").astype(jnp.float32),
        lax.psum(grad_w_value.astype(jnp.bfloat16), "dp").astype(jnp.float32),
        lax.psum(grad_w_out.astype(jnp.bfloat16), "dp").astype(jnp.float32),
        lax.psum(grad_w_gate.astype(jnp.bfloat16), "dp").astype(jnp.float32),
        lax.psum(grad_w_up.astype(jnp.bfloat16), "dp").astype(jnp.float32),
        lax.psum(grad_w_down.astype(jnp.bfloat16), "dp").astype(jnp.float32),
    )
    return (
        output,
        grad_tokens,
        grad_norm_attn,
        grad_w_query,
        grad_w_key,
        grad_w_value,
        grad_w_out,
        grad_norm_mlp,
        grad_w_gate,
        grad_w_up,
        grad_w_down,
    )


def solution(mesh):
    in_specs = (
        P(("dp", "tensor"), None),
        P("dp"),
        P("dp"),
        P(),
        P(None, "tensor"),
        P(None, "tensor"),
        P(None, "tensor"),
        P("tensor", None),
        P(),
        P(None, "tensor"),
        P(None, "tensor"),
        P("tensor", None),
        P(("dp", "tensor"), None),
    )
    out_specs = (
        P(("dp", "tensor"), None),
        P(("dp", "tensor"), None),
        P(),
        P(None, "tensor"),
        P(None, "tensor"),
        P(None, "tensor"),
        P("tensor", None),
        P(),
        P(None, "tensor"),
        P(None, "tensor"),
        P("tensor", None),
    )
    return jax.shard_map(body, mesh=mesh, in_specs=in_specs, out_specs=out_specs, check_vma=False)
```

profile of v0, /device:TPU:0, one launch (start us, length us, event | category | flops | bytes accessed | tf_op | source)
XLA Modules:
  0.0 1461.6 jit_solution(5925052065785356915)
XLA Ops:
  15.7 46.3 %all-gather.5.cloned.1.call-done = bf16[2048,1536]{1,0:T(8,128)(2,1)} async-done(((bf16[512,1536]{1,0:T(8,128)(2,1)}), bf16[2048,1536]{1,0:T(8,128)(2,1)}) %all-gather.5.cloned.1.call-update) | async-done | bytes 6291472 | tf_op jit(solution)/shard_map/all_gather | solution.py:104
  89.8 66.6 %while.28 = (s32[]{:T(128)}, bf16[4,512,2,2,96]{1,4,3,2,0:T(8,128)(2,1)}, f32[4,2,2,512]{3,2,1,0:T(2,128)}, s32[4,512]{1,0:T(4,128)S(1)}, s32[2048]{0:T(1024)S(1...) while((s32[]{:T(128)}, ...), condition=%wide.region_4.5_spmd.clone, body=%wide.region_1.4_spmd.clone.sunk | while | flops 1664284672 | bytes 60117144 | solution.py:135
  167.2 99.1 %reduce-scatter.5.cloned.1.call-done = f32[512,1536]{1,0:T(8,128)} async-done(((f32[2048,1536]{1,0:T(8,128)}), f32[512,1536]{1,0:T(8,128)}) %reduce-scatter.5.cloned.1.call-update) | async-done | bytes 3145744 | tf_op jit(solution)/shard_map/reduce_scatter | solution.py:138
  273.0 45.9 %all-gather.7.cloned.1.call-done = bf16[2048,1536]{1,0:T(8,128)(2,1)} async-done(((bf16[512,1536]{1,0:T(8,128)(2,1)}), bf16[2048,1536]{1,0:T(8,128)(2,1)}) %all-gather.7.cloned.1.call-update) | async-done | bytes 6291472 | tf_op jit(solution)/shard_map/all_gather | solution.py:148
  318.9 12.6 fusion.74
  340.3 26.4 %all-gather.9.cloned.1.call-done = bf16[2048,1536]{1,0:T(8,128)(2,1)} async-done(((bf16[512,1536]{1,0:T(8,128)(2,1)}), bf16[2048,1536]{1,0:T(8,128)(2,1)}) %all-gather.9.cloned.1.call-update) | async-done | bytes 6291472 | tf_op jit(solution)/shard_map/all_gather | solution.py:162
  366.8 18.8 %multiply_convert_fusion = (bf16[2048,1024]{1,0:T(8,128)(2,1)}, bf16[2048,1024]{1,0:T(8,128)(2,1)}, bf16[2048,1024]{1,0:T(8,128)(2,1)}) fusion(f32[2048,1024]{1,0:T(8,128)} %fusion.73, f32[2048,1024]{1,0:T(8,128)} %fusion.74, bf16[2048,1536]{1,0:T(8,128)(2,1)} %all-gather.9.cloned.1.call-done, bf16[1024,1536]{1,0:T(8,128)(2,1)S(1)} %copy-done), kind=kOutput, calls=%fused_computation.69 | convolution fusion | flops 6473908224 | bytes 38797312 | tf_op jit(solution)/shard_map/dot_general | solution.py:61
  397.2 12.9 convolution_add_fusion
  410.1 99.1 %reduce-scatter.9.cloned.1.call-done = f32[512,1536]{1,0:T(8,128)} async-done(((f32[2048,1536]{1,0:T(8,128)}), f32[512,1536]{1,0:T(8,128)}) %reduce-scatter.9.cloned.1.call-update) | async-done | bytes 3145744 | tf_op jit(solution)/shard_map/reduce_scatter | solution.py:171
  517.6 46.5 %all-gather.11.cloned.1.call-done = bf16[2048,1536]{1,0:T(8,128)(2,1)} async-done(((bf16[512,1536]{1,0:T(8,128)(2,1)}), bf16[2048,1536]{1,0:T(8,128)(2,1)}) %all-gather.11.cloned.1.call-update) | async-done | bytes 6291472 | tf_op jit(solution)/shard_map/all_gather | solution.py:181
  584.7 274.0 %while.29 = (s32[]{:T(128)}, f32[2048,2,96]{0,2,1:T(8,128)}, f32[2048,2,96]{0,2,1:T(8,128)}, f32[4,512,2,2,96]{1,0,4,3,2:T(4,128)}, bf16[4,512,2,2,96]{1,4,3,2,0...) while((s32[]{:T(128)}, f32[2048,2,96]{0,2,1:T(8,128)}, ...), condition=%wide.region_12.13_spmd.clone, body=%wide.region_10.12_spmd.clone.sunk | while | flops 4094752768 | bytes 214511840 | solution.py:222
  603.6 12.6 fusion.155
  636.6 16.1 %dynamic_update_slice.22 = f32[4,512,2,2,96]{1,0,4,3,2:T(4,128)} dynamic-update-slice(f32[4,512,2,2,96]{1,0,4,3,2:T(4,128)} %get-tuple-element.503, f32[1,512,2,2,96]{1,0,4,3,2:T(1,128)} %copy.49, s32[]{:T(128)S(6)} %copy.66, s32[]{:T(128)} %constant.58.clone.1..sunk, s32[]{:T(128)} %constant.58.clone.1..sunk, s32[]{:T(128)} %constant.58.clone.1..sunk, s32[]{:T(128)} %constant.58.clone.1..sunk) | dynamic-update-slice | bytes 1572868 | tf_op jit(solution)/shard_map/while/body/jit(dynamic_update_index_in_dim)/dynamic_update_slice | solution.py:222
  671.7 12.6 fusion.155
  684.3 12.2 fusion.156
  705.2 16.1 %dynamic_update_slice.22 = f32[4,512,2,2,96]{1,0,4,3,2:T(4,128)} dynamic-update-slice(f32[4,512,2,2,96]{1,0,4,3,2:T(4,128)} %get-tuple-element.503, f32[1,512,2,2,96]{1,0,4,3,2:T(1,128)} %copy.49, s32[]{:T(128)S(6)} %copy.66, s32[]{:T(128)} %constant.58.clone.1..sunk, s32[]{:T(128)} %constant.58.clone.1..sunk, s32[]{:T(128)} %constant.58.clone.1..sunk, s32[]{:T(128)} %constant.58.clone.1..sunk) | dynamic-update-slice | bytes 1572868 | tf_op jit(solution)/shard_map/while/body/jit(dynamic_update_index_in_dim)/dynamic_update_slice | solution.py:222
  740.3 12.6 fusion.155
  773.8 16.1 %dynamic_update_slice.22 = f32[4,512,2,2,96]{1,0,4,3,2:T(4,128)} dynamic-update-slice(f32[4,512,2,2,96]{1,0,4,3,2:T(4,128)} %get-tuple-element.503, f32[1,512,2,2,96]{1,0,4,3,2:T(1,128)} %copy.49, s32[]{:T(128)S(6)} %copy.66, s32[]{:T(128)} %constant.58.clone.1..sunk, s32[]{:T(128)} %constant.58.clone.1..sunk, s32[]{:T(128)} %constant.58.clone.1..sunk, s32[]{:T(128)} %constant.58.clone.1..sunk) | dynamic-update-slice | bytes 1572868 | tf_op jit(solution)/shard_map/while/body/jit(dynamic_update_index_in_dim)/dynamic_update_slice | solution.py:222
  809.0 12.6 fusion.155
  842.5 16.1 %dynamic_update_slice.22 = f32[4,512,2,2,96]{1,0,4,3,2:T(4,128)} dynamic-update-slice(f32[4,512,2,2,96]{1,0,4,3,2:T(4,128)} %get-tuple-element.503, f32[1,512,2,2,96]{1,0,4,3,2:T(1,128)} %copy.49, s32[]{:T(128)S(6)} %copy.66, s32[]{:T(128)} %constant.58.clone.1..sunk, s32[]{:T(128)} %constant.58.clone.1..sunk, s32[]{:T(128)} %constant.58.clone.1..sunk, s32[]{:T(128)} %constant.58.clone.1..sunk) | dynamic-update-slice | bytes 1572868 | tf_op jit(solution)/shard_map/while/body/jit(dynamic_update_index_in_dim)/dynamic_update_slice | solution.py:222
  883.0 12.8 add_convert_fusion
  957.3 40.1 %all-reduce = (f32[1536]{0:T(1024)}, f32[1536]{0:T(1024)}) all-reduce(f32[1536]{0:T(1024)S(1)} %get-tuple-element.234, f32[1536]{0:T(1024)S(1)} %copy-done.41), channel_id=1, replica_groups=mesh['dp'=8,'tensor'=4] {'dp','tensor'}, use_global_device_ids=true, to_apply=%region_16.17 | all-reduce | flops 3072 | bytes 24576 | tf_op jit(solution)/shard_map/psum | solution.py:254
  997.4 19.3 %reduce-scatter.7.cloned.1.call-done = bf16[512,1536]{1,0:T(8,128)(2,1)} async-done(((bf16[2048,1536]{1,0:T(8,128)(2,1)}), bf16[512,1536]{1,0:T(8,128)(2,1)}) %reduce-scatter.7.cloned.1.call-update) | async-done | bytes 1572880 | tf_op jit(solution)/shard_map/reduce_scatter | solution.py:155
  1023.7 413.4 %all-reduce.4.cloned.1.call-done = (bf16[1536,384]{1,0:T(8,128)(2,1)}, bf16[1536,192]{0,1:T(8,128)(2,1)}, bf16[1536,192]{0,1:T(8,128)(2,1)}, bf16[384,1536]{1,0:...) async-done(((bf16[1536,384]{1,0:T(8,128)(2,1)}, bf16[1536,192]{0,1:T(8,128)(2,1)}, bf16[1536,192]{0,1:T(8,128)(2,1)}, ...) | async-done | bytes 12976144 | tf_op jit(solution)/shard_map/psum | solution.py:256
  (284 shorter events, 425.3 us)
Async XLA Ops:
  7.2 359.6 %copy-start = (bf16[1024,1536]{1,0:T(8,128)(2,1)S(1)}, bf16[1024,1536]{1,0:T(8,128)(2,1)}, u32[]{:S(2)}) copy-start(bf16[1024,1536]{1,0:T(8,128)(2,1)} %param.28) | copy-start | bytes 9437188
  7.2 54.8 %all-gather.5.cloned.1.call-start = ((), (), s32[]{:S(2)}) async-start(), calls=%async_computation.4 | async-start | bytes 7864320 | tf_op jit(solution)/shard_map/all_gather | solution.py:104
  12.8 253.6 %reduce-scatter.5.cloned.1.call-start = ((), (), s32[]{:S(2)}) async-start(), calls=%async_computation.5 | async-start | bytes 15728640 | tf_op jit(solution)/shard_map/reduce_scatter | solution.py:138
  15.7 55.7 %copy-start.7 = (f32[2048,48]{0,1:T(8,128)}, f32[2048,48]{0,1:T(8,128)S(1)}, u32[]{:S(2)}) copy-start(f32[2048,48]{0,1:T(8,128)S(1)} %get-tuple-element.310) | copy-start | bytes 1179652
  167.2 103.7 %copy-start.35 = (f32[1536]{0:T(1024)S(1)}, f32[1536]{0:T(1024)}, u32[]{:S(2)}) copy-start(f32[1536]{0:T(1024)} %param.25) | copy-start | bytes 18436
  167.2 151.7 %all-gather.7.cloned.1.call-start = ((), (), s32[]{:S(2)}) async-start(), calls=%async_computation.6 | async-start | bytes 7864320 | tf_op jit(solution)/shard_map/all_gather | solution.py:148
  269.2 244.4 %copy-start.39 = (f32[512]{0:T(512)}, f32[512]{0:T(512)S(1)}, u32[]{:S(2)}) copy-start(f32[512]{0:T(512)S(1)} %add_rsqrt_fusion) | copy-start | bytes 6148
  272.4 94.4 %all-gather.9.cloned.1.call-start = ((), (), s32[]{:S(2)}) async-start(), calls=%async_computation.8 | async-start | bytes 7864320 | tf_op jit(solution)/shard_map/all_gather | solution.py:162
  273.0 236.3 %reduce-scatter.9.cloned.1.call-start = ((), (), s32[]{:S(2)}) async-start(), calls=%async_computation.9 | async-start | bytes 15728640 | tf_op jit(solution)/shard_map/reduce_scatter | solution.py:171
  318.9 12.6 copy-start.48
  318.9 12.6 copy-start.49
  366.8 18.8 %copy-start.50 = (bf16[1536,1024]{1,0:T(8,128)(2,1)S(1)}, bf16[1536,1024]{1,0:T(8,128)(2,1)}, u32[]{:S(2)}) copy-start(bf16[1536,1024]{1,0:T(8,128)(2,1)} %param.26) | copy-start | bytes 9437188
  410.1 154.0 %all-gather.11.cloned.1.call-start = ((), (), s32[]{:S(2)}) async-start(), calls=%async_computation.10 | async-start | bytes 7864320 | tf_op jit(solution)/shard_map/all_gather | solution.py:181
  517.5 436.8 %reduce-scatter.11.cloned.1.call-start = ((), (), s32[]{:S(2)}) async-start(), calls=%async_computation.11 | async-start | bytes 7864320 | tf_op jit(solution)/shard_map/reduce_scatter | solution.py:242
  616.2 12.2 copy-start.2
  684.3 12.2 copy-start.2
  868.4 14.7 %copy-start.20 = (bf16[2048,2,96]{0,2,1:T(8,128)(2,1)}, bf16[2048,2,96]{0,2,1:T(8,128)(2,1)S(1)}, u32[]{:S(2)}) copy-start(bf16[2048,2,96]{0,2,1:T(8,128)(2,1)S(1)} %convert_element_type.138) | copy-start | bytes 2359300
  895.8 120.9 %reduce-scatter.7.cloned.1.call-start = ((), (), s32[]{:S(2)}) async-start(), calls=%async_computation.7 | async-start | bytes 7864320 | tf_op jit(solution)/shard_map/reduce_scatter | solution.py:155
  906.8 530.3 %all-reduce.4.cloned.1.call-start = ((), (), s32[]{:S(2)}) async-start(), calls=%async_computation.12 | async-start | bytes 25952256 | tf_op jit(solution)/shard_map/psum | solution.py:256
  906.9 22.2 %slice-start.2 = ((s8[6291456]{0:T(1024)(128)(4,1)}), s8[4194304]{0:T(1024)(128)(4,1)S(1)}, s32[]{:S(2)}) async-start(s8[6291456]{0:T(1024)(128)(4,1)} %bitcast.262), calls=%async_computation.15 | async-start | bytes 8388608
  918.9 18.7 %slice-start = ((s8[6291456]{0:T(1024)(128)(4,1)}), s8[4194304]{0:T(1024)(128)(4,1)S(1)}, s32[]{:S(2)}) async-start(s8[6291456]{0:T(1024)(128)(4,1)} %bitcast.260), calls=%async_computation.13 | async-start | bytes 8388608
  950.4 66.3 %copy-start.36 = (f32[1536]{0:T(1024)S(1)}, f32[1536]{0:T(1024)}, u32[]{:S(2)}) copy-start(f32[1536]{0:T(1024)} %param.25) | copy-start | bytes 18436
  950.4 66.3 %copy-start.40 = (f32[512]{0:T(512)S(1)}, f32[512]{0:T(512)}, u32[]{:S(2)}) copy-start(f32[512]{0:T(512)} %copy-done.39) | copy-start | bytes 6148
  950.4 66.3 %copy-start.45 = (f32[512]{0:T(512)S(1)}, f32[512]{0:T(512)}, u32[]{:S(2)}) copy-start(f32[512]{0:T(512)} %copy-done.44) | copy-start | bytes 6148
  (55 other events, 293.3 us)
Sparse Core Ops, SparseCore 0:
  12.9 49.0 all-gather.4
  167.3 99.0 reduce-scatter.4
  272.5 46.3 all-gather.6
  320.3 46.3 all-gather.8
  410.2 99.0 reduce-scatter.8
  517.7 46.3 all-gather.10
  895.9 58.3 reduce-scatter.10
  957.6 59.0 reduce-scatter.6
  1023.5 413.5 all-reduce.3
where the time goes:
time: 1470 us; the launch traced here: 1460 us
  waiting for transfers between devices  801 us (54%)
  matrix products  336 us (23%)
  other arithmetic  136 us (9%)
  local copies, waits for them, and re-layouts  132 us (9%)
  blocking collectives  40.1 us (3%)
  between operations  14.9 us (1%)
    psum x1, waiting for transfers between devices, body(): lax.psum(grad_w_query.astype(jnp.bfloat16), 'dp').astype(jnp.float32)  413 us
    reduce_scatter x1, waiting for transfers between devices, body(): lax.psum_scatter(contract_cols(grad_gate, w_gate) + contract_cols(grad_up...  99.1 us
    reduce_scatter x1, waiting for transfers between devices, body(): lax.psum_scatter(jnp.dot(row_slice, w_out, preferred_element_type=jnp.flo...  99.1 us
    dot_general x7, matrix products, contract_cols(): lax.dot_general(left, right, (((1,), (1,)), ((), ())), preferred_element_...  76.6 us
    dynamic_update_slice x8, local copies, waits for them, and re-layouts, body(): lax.scan(attend_back, (zero_state, zero_state), (blocks_of_query, grad_bl...  71.2 us
    dot_general x4, matrix products, attend_back(): jnp.einsum('qgrd,kgd->grqk', grad_block, heads_of_value, preferred_elemen...  50.6 us
    convert_element_type x4, other arithmetic, attend_back(): grad_scores = (weights * (grad_weights - inner_sum)).astype(jnp.bfloat16)  48.7 us
    all_gather x1, waiting for transfers between devices, body(): lax.all_gather(grad_hidden_one.astype(jnp.bfloat16), 'tensor', axis=0, ti...  46.5 us
  transfers between devices with their start and end apart: 9, of which 9 were waited for; matrix products, arithmetic and copies ran while one was open for 6% of the time, Pallas kernels for 0%

commit v1 on v0

--- a/solution.py
+++ b/solution.py
@@ -1,3 +1,4 @@
+import functools
 import math
 import jax
 import jax.numpy as jnp
@@ -8,6 +9,14 @@
 epsilon = 1e-05
 rope_base = 100000.0
 masked_value = -1e30
+
+
+def _read_sector(mine, axis_key):
+    w_next = lax.all_gather(mine, axis_key)
+    return jnp.sum(w_next, 0)
+
+
+zone_resolve = functools.partial(_read_sector, axis_key="dp")
 
 
 def angle_tables(positions, width):
@@ -253,7 +262,7 @@
     grad_tokens = grad_hidden_one + norm_back(grad_normed_one, norm_attn, unit_one, inverse_one)
     grad_norm_attn, grad_norm_mlp = lax.psum((grad_norm_attn, grad_norm_mlp), ("dp", "tensor"))
     grad_w_query, grad_w_key, grad_w_value, grad_w_out, grad_w_gate, grad_w_up, grad_w_down = (
-        lax.psum(grad_w_query.astype(jnp.bfloat16), "dp").astype(jnp.float32),
+        zone_resolve(grad_w_query.astype(jnp.bfloat16)).astype(jnp.float32),
         lax.psum(grad_w_key.astype(jnp.bfloat16), "dp").astype(jnp.float32),
         lax.psum(grad_w_value.astype(jnp.bfloat16), "dp").astype(jnp.float32),
         lax.psum(grad_w_out.astype(jnp.bfloat16), "dp").astype(jnp.float32),

time: 1470 us -> 1530 us (1.041)
  waiting for transfers between devices: 801 us -> 841 us
    all_gather x0 -> x1, waiting for transfers between devices: none -> 134 us  [_read_sector(): w_next = lax.all_gather(mine, axis_key)]
    psum x1, waiting for transfers between devices: 413 us -> 312 us  [body(): lax.psum(grad_w_key.astype(jnp.bfloat16), 'dp').astype(jnp.float32)]
    reduce_scatter x1, waiting for transfers between devices: 3.95 us -> 42 us  [body(): lax.psum_scatter((contract_cols(grad_q_proj, w_query) + contract_cols(gra...]
    all_gather x1, waiting for transfers between devices: 46.5 us -> 16.4 us  [body(): lax.all_gather(grad_hidden_one.astype(jnp.bfloat16), 'tensor', axis=0, ti...]
  transfers between devices with their start and end apart: 9 -> 10, of which waited for: 9 -> 10; matrix products, arithmetic and copies ran while one was open for 6% -> 9% of each run, Pallas kernels for 0% -> 0%
where the time goes in v1:
time: 1530 us; the launch traced here: 1520 us
  waiting for transfers between devices  841 us (55%)
  matrix products  343 us (22%)
  other arithmetic  147 us (10%)
  local copies, waits for them, and re-layouts  131 us (9%)
  blocking collectives  40 us (3%)
    psum x1, waiting for transfers between devices, body(): lax.psum(grad_w_key.astype(jnp.bfloat16), 'dp').astype(jnp.float32)  312 us
    all_gather x1, waiting for transfers between devices, _read_sector(): w_next = lax.all_gather(mine, axis_key)  134 us
    reduce_scatter x1, waiting for transfers between devices, body(): lax.psum_scatter(contract_cols(grad_gate, w_gate) + contract_cols(grad_up...  99.2 us
    reduce_scatter x1, waiting for transfers between devices, body(): lax.psum_scatter(jnp.dot(row_slice, w_out, preferred_element_type=jnp.flo...  99.1 us
    dot_general x7, matrix products, contract_cols(): lax.dot_general(left, right, (((1,), (1,)), ((), ())), preferred_element_...  77.2 us
    dynamic_update_slice x8, local copies, waits for them, and re-layouts, body(): lax.scan(attend_back, (zero_state, zero_state), (blocks_of_query, grad_bl...  71.2 us
    dot_general x4, matrix products, attend_back(): jnp.einsum('qgrd,kgd->grqk', grad_block, heads_of_value, preferred_elemen...  50.4 us
    dot_general x7, matrix products, contract_rows(): lax.dot_general(left, right, (((0,), (0,)), ((), ())), preferred_element_...  49.4 us
  transfers between devices with their start and end apart: 10, of which 10 were waited for; matrix products, arithmetic and copies ran while one was open for 9% of the time, Pallas kernels for 0%

profile of v1, /device:TPU:0, one launch (start us, length us, event | category | flops | bytes accessed | tf_op | source)
XLA Modules:
  0.0 1518.1 jit_solution(14227580577126438357)
XLA Ops:
  15.7 46.3 %all-gather.7.cloned.1.call-done = bf16[2048,1536]{1,0:T(8,128)(2,1)} async-done(((bf16[512,1536]{1,0:T(8,128)(2,1)}), bf16[2048,1536]{1,0:T(8,128)(2,1)}) %all-gather.7.cloned.1.call-update) | async-done | bytes 6291472 | tf_op jit(solution)/shard_map/all_gather | solution.py:113
  89.8 66.5 %while.28 = (s32[]{:T(128)}, bf16[4,512,2,2,96]{1,4,3,2,0:T(8,128)(2,1)}, f32[4,2,2,512]{3,2,1,0:T(2,128)}, s32[4,512]{1,0:T(4,128)S(1)}, s32[2048]{0:T(1024)S(1...) while((s32[]{:T(128)}, ...), condition=%wide.region_4.5_spmd.clone, body=%wide.region_1.4_spmd.clone.sunk | while | flops 1664284672 | bytes 60117144 | solution.py:144
  167.1 99.1 %reduce-scatter.5.cloned.1.call-done = f32[512,1536]{1,0:T(8,128)} async-done(((f32[2048,1536]{1,0:T(8,128)}), f32[512,1536]{1,0:T(8,128)}) %reduce-scatter.5.cloned.1.call-update) | async-done | bytes 3145744 | tf_op jit(solution)/shard_map/reduce_scatter | solution.py:147
  272.9 45.9 %all-gather.9.cloned.1.call-done = bf16[2048,1536]{1,0:T(8,128)(2,1)} async-done(((bf16[512,1536]{1,0:T(8,128)(2,1)}), bf16[2048,1536]{1,0:T(8,128)(2,1)}) %all-gather.9.cloned.1.call-update) | async-done | bytes 6291472 | tf_op jit(solution)/shard_map/all_gather | solution.py:157
  340.2 26.4 %all-gather.11.cloned.1.call-done = bf16[2048,1536]{1,0:T(8,128)(2,1)} async-done(((bf16[512,1536]{1,0:T(8,128)(2,1)}), bf16[2048,1536]{1,0:T(8,128)(2,1)}) %all-gather.11.cloned.1.call-update) | async-done | bytes 6291472 | tf_op jit(solution)/shard_map/all_gather | solution.py:171
  366.7 18.8 %multiply_convert_fusion = (bf16[2048,1024]{1,0:T(8,128)(2,1)}, bf16[2048,1024]{1,0:T(8,128)(2,1)}, bf16[2048,1024]{1,0:T(8,128)(2,1)}) fusion(f32[2048,1024]{1,0:T(8,128)} %fusion.73, f32[2048,1024]{1,0:T(8,128)} %fusion.74, bf16[2048,1536]{1,0:T(8,128)(2,1)} %all-gather.11.cloned.1.call-done, bf16[1024,1536]{1,0:T(8,128)(2,1)S(1)} %copy-done), kind=kOutput, calls=%fused_computation.69 | convolution fusion | flops 6473908224 | bytes 38797312 | tf_op jit(solution)/shard_map/dot_general | solution.py:70
  397.4 13.1 convolution_add_fusion
  410.6 99.2 %reduce-scatter.9.cloned.1.call-done = f32[512,1536]{1,0:T(8,128)} async-done(((f32[2048,1536]{1,0:T(8,128)}), f32[512,1536]{1,0:T(8,128)}) %reduce-scatter.9.cloned.1.call-update) | async-done | bytes 3145744 | tf_op jit(solution)/shard_map/reduce_scatter | solution.py:180
  548.1 16.4 %all-gather.13.cloned.1.call-done = bf16[2048,1536]{1,0:T(8,128)(2,1)} async-done(((bf16[512,1536]{1,0:T(8,128)(2,1)}), bf16[2048,1536]{1,0:T(8,128)(2,1)}) %all-gather.13.cloned.1.call-update) | async-done | bytes 6291472 | tf_op jit(solution)/shard_map/all_gather | solution.py:190
  585.2 273.6 %while.29 = (s32[]{:T(128)}, f32[2048,2,96]{0,2,1:T(8,128)}, f32[2048,2,96]{0,2,1:T(8,128)}, f32[4,512,2,2,96]{1,0,4,3,2:T(4,128)}, bf16[4,512,2,2,96]{1,4,3,2,0...) while((s32[]{:T(128)}, f32[2048,2,96]{0,2,1:T(8,128)}, ...), condition=%wide.region_12.13_spmd.clone, body=%wide.region_10.12_spmd.clone.sunk | while | flops 4094752768 | bytes 214511840 | solution.py:231
  604.0 12.6 fusion.155
  637.0 16.1 %dynamic_update_slice.22 = f32[4,512,2,2,96]{1,0,4,3,2:T(4,128)} dynamic-update-slice(f32[4,512,2,2,96]{1,0,4,3,2:T(4,128)} %get-tuple-element.502, f32[1,512,2,2,96]{1,0,4,3,2:T(1,128)} %copy.49, s32[]{:T(128)S(6)} %copy.66, s32[]{:T(128)} %constant.59.clone.1..sunk, s32[]{:T(128)} %constant.59.clone.1..sunk, s32[]{:T(128)} %constant.59.clone.1..sunk, s32[]{:T(128)} %constant.59.clone.1..sunk) | dynamic-update-slice | bytes 1572868 | tf_op jit(solution)/shard_map/while/body/jit(dynamic_update_index_in_dim)/dynamic_update_slice | solution.py:231
  672.0 12.6 fusion.155
  705.5 16.1 %dynamic_update_slice.22 = f32[4,512,2,2,96]{1,0,4,3,2:T(4,128)} dynamic-update-slice(f32[4,512,2,2,96]{1,0,4,3,2:T(4,128)} %get-tuple-element.502, f32[1,512,2,2,96]{1,0,4,3,2:T(1,128)} %copy.49, s32[]{:T(128)S(6)} %copy.66, s32[]{:T(128)} %constant.59.clone.1..sunk, s32[]{:T(128)} %constant.59.clone.1..sunk, s32[]{:T(128)} %constant.59.clone.1..sunk, s32[]{:T(128)} %constant.59.clone.1..sunk) | dynamic-update-slice | bytes 1572868 | tf_op jit(solution)/shard_map/while/body/jit(dynamic_update_index_in_dim)/dynamic_update_slice | solution.py:231
  740.6 12.6 fusion.155
  774.0 16.1 %dynamic_update_slice.22 = f32[4,512,2,2,96]{1,0,4,3,2:T(4,128)} dynamic-update-slice(f32[4,512,2,2,96]{1,0,4,3,2:T(4,128)} %get-tuple-element.502, f32[1,512,2,2,96]{1,0,4,3,2:T(1,128)} %copy.49, s32[]{:T(128)S(6)} %copy.66, s32[]{:T(128)} %constant.59.clone.1..sunk, s32[]{:T(128)} %constant.59.clone.1..sunk, s32[]{:T(128)} %constant.59.clone.1..sunk, s32[]{:T(128)} %constant.59.clone.1..sunk) | dynamic-update-slice | bytes 1572868 | tf_op jit(solution)/shard_map/while/body/jit(dynamic_update_index_in_dim)/dynamic_update_slice | solution.py:231
  809.1 12.6 fusion.155
  842.6 16.1 %dynamic_update_slice.22 = f32[4,512,2,2,96]{1,0,4,3,2:T(4,128)} dynamic-update-slice(f32[4,512,2,2,96]{1,0,4,3,2:T(4,128)} %get-tuple-element.502, f32[1,512,2,2,96]{1,0,4,3,2:T(1,128)} %copy.49, s32[]{:T(128)S(6)} %copy.66, s32[]{:T(128)} %constant.59.clone.1..sunk, s32[]{:T(128)} %constant.59.clone.1..sunk, s32[]{:T(128)} %constant.59.clone.1..sunk, s32[]{:T(128)} %constant.59.clone.1..sunk) | dynamic-update-slice | bytes 1572868 | tf_op jit(solution)/shard_map/while/body/jit(dynamic_update_index_in_dim)/dynamic_update_slice | solution.py:231
  895.0 12.7 add_convert_fusion
  926.9 312.3 %all-reduce.4.cloned.1.call-done = (bf16[1536,192]{0,1:T(8,128)(2,1)}, bf16[1536,192]{0,1:T(8,128)(2,1)}, bf16[384,1536]{1,0:T(8,128)(2,1)}, bf16[1536,1024]{1,0...) async-done(((bf16[1536,192]{0,1:T(8,128)(2,1)}, bf16[1536,192]{0,1:T(8,128)(2,1)}, bf16[384,1536]{1,0:T(8,128)(2,1)}, bf16[1536,1024]{1,0:T(8,128)(2,1)}, ...) | async-done | bytes 11796496 | tf_op jit(solution)/shard_map/psum | solution.py:266
  1257.2 42.0 %reduce-scatter.11.cloned.1.call-done = bf16[512,1536]{1,0:T(8,128)(2,1)} async-done(((bf16[2048,1536]{1,0:T(8,128)(2,1)}), bf16[512,1536]{1,0:T(8,128)(2,1)}) %reduce-scatter.11.cloned.1.call-update) | async-done | bytes 1572880 | tf_op jit(solution)/shard_map/reduce_scatter | solution.py:251
  1302.2 40.0 %all-reduce = (f32[1536]{0:T(1024)}, f32[1536]{0:T(1024)}) all-reduce(f32[1536]{0:T(1024)S(1)} %get-tuple-element.234, f32[1536]{0:T(1024)S(1)} %copy-done.37), channel_id=1, replica_groups=mesh['dp'=8,'tensor'=4] {'dp','tensor'}, use_global_device_ids=true, to_apply=%region_16.17 | all-reduce | flops 3072 | bytes 24576 | tf_op jit(solution)/shard_map/psum | solution.py:263
  1342.2 18.7 %reduce-scatter.7.cloned.1.call-done = bf16[512,1536]{1,0:T(8,128)(2,1)} async-done(((bf16[2048,1536]{1,0:T(8,128)(2,1)}), bf16[512,1536]{1,0:T(8,128)(2,1)}) %reduce-scatter.7.cloned.1.call-update) | async-done | bytes 1572880 | tf_op jit(solution)/shard_map/reduce_scatter | solution.py:164
  1367.8 134.0 %all-gather.15.cloned.1.call-done = bf16[12288,384]{1,0:T(8,128)(2,1)} async-done(((bf16[1536,384]{1,0:T(8,128)(2,1)}), bf16[12288,384]{1,0:T(8,128)(2,1)}) %all-gather.15.cloned.1.call-update) | async-done | bytes 9437200 | tf_op jit(solution)/shard_map/all_gather | solution.py:15
  (275 shorter events, 462.4 us)
Async XLA Ops:
  7.2 359.5 %copy-start = (bf16[1024,1536]{1,0:T(8,128)(2,1)S(1)}, bf16[1024,1536]{1,0:T(8,128)(2,1)}, u32[]{:S(2)}) copy-start(bf16[1024,1536]{1,0:T(8,128)(2,1)} %param.28) | copy-start | bytes 9437188
  7.2 54.8 %all-gather.7.cloned.1.call-start = ((), (), s32[]{:S(2)}) async-start(), calls=%async_computation.4 | async-start | bytes 7864320 | tf_op jit(solution)/shard_map/all_gather | solution.py:113
  12.8 253.5 %reduce-scatter.5.cloned.1.call-start = ((), (), s32[]{:S(2)}) async-start(), calls=%async_computation.5 | async-start | bytes 15728640 | tf_op jit(solution)/shard_map/reduce_scatter | solution.py:147
  15.7 55.7 %copy-start.7 = (f32[2048,48]{0,1:T(8,128)}, f32[2048,48]{0,1:T(8,128)S(1)}, u32[]{:S(2)}) copy-start(f32[2048,48]{0,1:T(8,128)S(1)} %get-tuple-element.309) | copy-start | bytes 1179652
  167.1 103.8 %copy-start.31 = (f32[1536]{0:T(1024)S(1)}, f32[1536]{0:T(1024)}, u32[]{:S(2)}) copy-start(f32[1536]{0:T(1024)} %param.25) | copy-start | bytes 18436
  167.1 151.8 %all-gather.9.cloned.1.call-start = ((), (), s32[]{:S(2)}) async-start(), calls=%async_computation.6 | async-start | bytes 7864320 | tf_op jit(solution)/shard_map/all_gather | solution.py:157
  269.1 245.0 %copy-start.35 = (f32[512]{0:T(512)}, f32[512]{0:T(512)S(1)}, u32[]{:S(2)}) copy-start(f32[512]{0:T(512)S(1)} %add_rsqrt_fusion) | copy-start | bytes 6148
  272.3 94.4 %all-gather.11.cloned.1.call-start = ((), (), s32[]{:S(2)}) async-start(), calls=%async_computation.8 | async-start | bytes 7864320 | tf_op jit(solution)/shard_map/all_gather | solution.py:171
  272.9 236.9 %reduce-scatter.9.cloned.1.call-start = ((), (), s32[]{:S(2)}) async-start(), calls=%async_computation.9 | async-start | bytes 15728640 | tf_op jit(solution)/shard_map/reduce_scatter | solution.py:180
  318.8 12.6 copy-start.44
  318.8 12.6 copy-start.45
  366.7 18.8 %copy-start.46 = (bf16[1536,1024]{1,0:T(8,128)(2,1)S(1)}, bf16[1536,1024]{1,0:T(8,128)(2,1)}, u32[]{:S(2)}) copy-start(bf16[1536,1024]{1,0:T(8,128)(2,1)} %param.26) | copy-start | bytes 9437188
  410.5 154.0 %all-gather.13.cloned.1.call-start = ((), (), s32[]{:S(2)}) async-start(), calls=%async_computation.10 | async-start | bytes 7864320 | tf_op jit(solution)/shard_map/all_gather | solution.py:190
  518.0 721.1 %all-reduce.4.cloned.1.call-start = ((), (), s32[]{:S(2)}) async-start(), calls=%async_computation.13 | async-start | bytes 23592960 | tf_op jit(solution)/shard_map/psum | solution.py:266
  518.1 21.6 %slice-start.2 = ((s8[6291456]{0:T(1024)(128)(4,1)}), s8[4194304]{0:T(1024)(128)(4,1)S(1)}, s32[]{:S(2)}) async-start(s8[6291456]{0:T(1024)(128)(4,1)} %bitcast.264), calls=%async_computation.16 | async-start | bytes 8388608
  873.1 426.1 %reduce-scatter.11.cloned.1.call-start = ((), (), s32[]{:S(2)}) async-start(), calls=%async_computation.11 | async-start | bytes 7864320 | tf_op jit(solution)/shard_map/reduce_scatter | solution.py:251
  907.8 453.0 %reduce-scatter.7.cloned.1.call-start = ((), (), s32[]{:S(2)}) async-start(), calls=%async_computation.7 | async-start | bytes 7864320 | tf_op jit(solution)/shard_map/reduce_scatter | solution.py:164
  919.0 582.8 %all-gather.15.cloned.1.call-start = ((), (), s32[]{:S(2)}) async-start(), calls=%async_computation.12 | async-start | bytes 10616832 | tf_op jit(solution)/shard_map/all_gather | solution.py:15
  1253.6 45.6 %copy-start.34 = (f32[1536]{0:T(1024)S(1)}, f32[1536]{0:T(1024)}, u32[]{:S(2)}) copy-start(f32[1536]{0:T(1024)} %param.20) | copy-start | bytes 18436
  1253.6 45.6 %copy-start.39 = (f32[512]{0:T(512)S(1)}, f32[512]{0:T(512)}, u32[]{:S(2)}) copy-start(f32[512]{0:T(512)} %copy-done.38) | copy-start | bytes 6148
  1257.2 44.9 %copy-start.37 = (f32[1536]{0:T(1024)S(1)}, f32[1536]{0:T(1024)}, u32[]{:S(2)}) copy-start(f32[1536]{0:T(1024)} %get-tuple-element.232) | copy-start | bytes 18436
  1257.2 103.6 %copy-start.32 = (f32[1536]{0:T(1024)S(1)}, f32[1536]{0:T(1024)}, u32[]{:S(2)}) copy-start(f32[1536]{0:T(1024)} %param.25) | copy-start | bytes 18436
  1257.2 103.6 %copy-start.36 = (f32[512]{0:T(512)S(1)}, f32[512]{0:T(512)}, u32[]{:S(2)}) copy-start(f32[512]{0:T(512)} %copy-done.35) | copy-start | bytes 6148
  1257.2 103.6 %copy-start.41 = (f32[512]{0:T(512)S(1)}, f32[512]{0:T(512)}, u32[]{:S(2)}) copy-start(f32[512]{0:T(512)} %copy-done.40) | copy-start | bytes 6148
  (50 other events, 299.7 us)
Sparse Core Ops, SparseCore 0:
  12.9 49.0 all-gather.6
  167.2 99.0 reduce-scatter.4
  272.4 46.3 all-gather.8
  320.3 46.3 all-gather.10
  410.7 99.0 reduce-scatter.8
  518.2 46.3 all-gather.12
  873.2 365.8 all-reduce.3
  1241.9 57.2 reduce-scatter.10
  1301.7 59.0 reduce-scatter.6
  1363.7 138.0 all-gather.14
